TPU v7x, 32 devices: a whole 2x2x4 slice. The times are simulated.
32 devices in a mesh: tok: 8 (over z, x), head: 4 (over y, core).
Axes of the slice: x: 2, y: 2, z: 4, core: 2. Of those that a mesh axis runs over, the one named last changes fastest.
Arguments:
- queries: bfloat16 [1024, 2048], P('tok', 'head'), may hold values from -32 to 32, as said below
- key_rows: bfloat16 [1024, 2048], P('tok', 'head'), may hold values from -16 to 16
- value_rows: bfloat16 [1024, 2048], P('tok', 'head'), may hold values from -6 to 6
- learn_rates: float32 [1024, 4], P('tok', 'head'), may hold values from 0.25 to 12, as said below
- fast_weights: bfloat16 [4, 3, 512, 512], P('head'), may hold values from -0.25 to 0.25
- out_weight: bfloat16 [2048, 2048], P(None, 'head'), may hold values from -0.5 to 0.5
Outputs:
- layer_out: bfloat16 [1024, 2048], P('tok', 'head')
Inputs may be any that keep to these rules, and one draw needn't show every extreme that they name: `queries`: queries drawn together with the keys. `learn_rates`: Positive.
All inputs are finite; a program needn't handle non-finite values.
Results may differ from a plain program's by a relative error of at most 0.019.
Values may be sent and summed in bfloat16 or wider, within the bound.
A program may use at most 64 MiB of HBM per device.

v0:
```python
import functools

import jax
import jax.numpy as jnp
from jax import lax
from jax.experimental import pallas as pl
from jax.experimental.pallas import tpu as pltpu
from jax.sharding import PartitionSpec as P

HD = 512
WIN = 1024
NS_STEPS = 2
PAIR = 2


ns_first = 3.4445
ns_second = -4.775
ns_third = 2.0315
update_rate = 2.0
fw_scale = 0.5
eps = 1e-06

MESH = pl.DeviceIdType.MESH


def passed_along(block, axis, distance):
    devices = range(lax.axis_size(axis))
    route = [(i - distance, i) for i in devices if i - distance in devices]
    return lax.ppermute(block, axis, route)


def rms_norm(values):
    values = values.astype(jnp.float32)
    return values * lax.rsqrt(jnp.mean(values * values, axis=-1, keepdims=True) + eps)


def contract_first(left, right):
    return lax.dot_general(
        left, right, (((0,), (0,)), ((), ())), preferred_element_type=jnp.float32
    )


def contract_last(left, right):
    return lax.dot_general(
        left, right, (((1,), (1,)), ((), ())), preferred_element_type=jnp.float32
    )


def matmul(left, right):
    return jnp.dot(left, right, preferred_element_type=jnp.float32)


def block_orders(depth):
    orders = []
    for z in range(depth):
        waiting = []
        for zp in range(depth):
            apart = abs(z - zp)
            waiting.append((2 * apart, zp * 2 + 1, max(0, 2 * apart - 1)))
            waiting.append((2 * apart + 2, zp * 2, 2 * apart + 1))
        order = []
        for t in range(2 * depth):
            ready = [entry for entry in waiting if entry[2] <= t]
            best = min(ready, key=lambda entry: (entry[0], -(entry[1] % 2), entry[1]))
            waiting.remove(best)
            order.append(best[1])
        orders.append(order)
    return orders


def fused_kernel(
    n_tok,
    q_hbm, k_hbm, v_hbm, rate_hbm, weights_hbm, out_hbm, result,
    q_ref, k_buf, v_buf, r_ref, w_ref, ow_ref,
    grads, ortho, gram_ref, cross_ref,
    top_ref, total_ref, acc_ref, heads_buf,
    local_sem, recv_sem, up_sem, down_sem, pair_sem,
    head_recv, head_send,
):
    rows, width = q_ref.shape
    depth = n_tok // PAIR
    me = lax.axis_index("tok")
    head = lax.axis_index("head")
    z = me // PAIR
    x = me % PAIR
    other = (PAIR - 1) - x
    core_peer = head + 1 - 2 * (head % 2)
    row_peer = (head + 2) % 4
    bufs = (k_buf, v_buf)
    panels = width // rows
    tail = panels * rows

    def local_copy(source, target, index):
        return pltpu.make_async_copy(source, target, local_sem.at[index])

    loads = [
        local_copy(k_hbm, k_buf.at[me], 0),
        local_copy(rate_hbm, r_ref, 1),
        local_copy(out_hbm, ow_ref, 2),
        local_copy(weights_hbm.at[0], w_ref, 3),
        local_copy(q_hbm, q_ref, 4),
    ]
    value_loads = [
        local_copy(
            v_hbm.at[:, pl.ds(panel * rows, rows)],
            v_buf.at[me, pl.ds(panel * rows, rows)],
            5 + panel,
        )
        for panel in range(panels)
    ]
    for load in value_loads + loads[:2] + loads[3:] + loads[2:3]:
        load.start()

    barrier = pltpu.get_barrier_semaphore()

    @pl.when(z > 0)
    def _():
        pl.semaphore_signal(barrier, inc=1, device_id={"tok": me - PAIR}, device_id_type=MESH)

    @pl.when(z < depth - 1)
    def _():
        pl.semaphore_signal(barrier, inc=1, device_id={"tok": me + PAIR}, device_id_type=MESH)

    pl.semaphore_signal(
        barrier, inc=1, device_id={"tok": z * PAIR + other}, device_id_type=MESH
    )
    pl.semaphore_signal(barrier, inc=1, device_id={"head": core_peer}, device_id_type=MESH)
    pl.semaphore_signal(barrier, inc=1, device_id={"head": row_peer}, device_id_type=MESH)
    has_lower = jnp.where(z > 0, 1, 0)
    has_upper = jnp.where(z < depth - 1, 1, 0)
    pl.semaphore_wait(barrier, 3 + has_lower + has_upper)

    def hop(slot, piece, sems, target, own=False):
        source = k_hbm if own else bufs[piece].at[slot]
        return pltpu.make_async_remote_copy(
            src_ref=source,
            dst_ref=bufs[piece].at[slot],
            send_sem=sems.at[slot, piece],
            recv_sem=recv_sem.at[slot, piece],
            device_id={"tok": target},
            device_id_type=MESH,
        )

    def each_hop(zp, piece, action, own=False):
        slot = zp * PAIR + x

        @pl.when((zp <= z) & (z < depth - 1))
        def _():
            action(hop(slot, piece, up_sem, me + PAIR, own))

        @pl.when((zp >= z) & (z > 0))
        def _():
            action(hop(slot, piece, down_sem, me - PAIR, own))

        def across():
            action(hop(slot, piece, pair_sem, z * PAIR + other, own))

        if piece == 1:
            pl.when((zp == z) | ((zp > 0) & (zp < depth - 1)))(across)
        else:
            across()

    def each_detour(zp, action):
        slot = zp * PAIR + other

        @pl.when((zp == 0) & (z < depth - 1))
        def _():
            action(hop(slot, 1, up_sem, me + PAIR))

        @pl.when((zp == depth - 1) & (z > 0))
        def _():
            action(hop(slot, 1, down_sem, me - PAIR))

    def start(copy):
        copy.start()

    def arrive(slot, piece):
        hop(slot, piece, pair_sem, z * PAIR + other).wait_recv()

    each_hop(z, 0, start, own=True)
    for load in value_loads:
        load.wait()
    loads[1].wait()
    rest = r_ref[...]
    digits = []
    for _ in range(3):
        digit = rest.astype(jnp.bfloat16)
        rest = rest - digit.astype(jnp.float32)
        digits.append(digit.astype(jnp.float32))
    digits.append(jnp.zeros((13, rows), jnp.float32))
    v_buf[me, tail:, :] = jnp.concatenate(digits, axis=0).astype(jnp.bfloat16)
    each_hop(z, 1, start)

    def value(slot):
        return jnp.concatenate(
            [v_buf[slot, panel * rows : (panel + 1) * rows, :] for panel in range(panels)],
            axis=1,
        )

    orders = block_orders(depth)

    def at_place(values, place):
        chosen = values[0]
        for index in range(1, len(values)):
            chosen = jnp.where(place == index, values[index], chosen)
        return chosen

    mine = [at_place([order[t] for order in orders], z) for t in range(n_tok)]

    grads[...] = jnp.zeros_like(grads)
    top_ref[...] = jnp.full_like(top_ref, -1e30)
    total_ref[...] = jnp.zeros_like(total_ref)
    acc_ref[...] = jnp.zeros_like(acc_ref)
    loads[0].wait()
    for load in loads[3:]:
        load.wait()

    def attend(slot):
        scores = contract_last(q_ref[...], k_buf[slot]) * HD ** (-0.5)
        row_ids = lax.broadcasted_iota(jnp.int32, scores.shape, 0) + me * rows
        col_ids = lax.broadcasted_iota(jnp.int32, scores.shape, 1) + slot * rows
        scores = jnp.where(col_ids <= row_ids, scores, -1e30)
        top = top_ref[:, :1]
        new_top = jnp.maximum(top, jnp.max(scores, axis=1, keepdims=True))
        fade = jnp.exp(top - new_top)
        shares = jnp.exp(scores - new_top)
        total = total_ref[:, :1] * fade + jnp.sum(shares, axis=1, keepdims=True)
        acc_ref[...] = acc_ref[...] * fade + matmul(shares.astype(jnp.bfloat16), value(slot))
        top_ref[...] = jnp.broadcast_to(new_top, top_ref.shape)
        total_ref[...] = jnp.broadcast_to(total, total_ref.shape)

    def learn(slot):
        key_norm = rms_norm(k_buf[slot]).astype(jnp.bfloat16)
        digits = v_buf[slot, tail:, :].astype(jnp.float32)
        rates = (digits[0:1] + digits[1:2]) + digits[2:3]
        rates = jnp.broadcast_to(rates, (rows, rows)).T[:, :1]
        scaled = (rates * value(slot).astype(jnp.float32)).astype(jnp.bfloat16)
        gate = matmul(key_norm, w_ref[0])
        up_part = matmul(key_norm, w_ref[1])
        back = contract_last(scaled, w_ref[2])
        sigmoid_gate = jax.nn.sigmoid(gate)
        activated = gate * sigmoid_gate
        hidden = (activated * up_part).astype(jnp.bfloat16)
        d_gate = (back * up_part * sigmoid_gate * (1.0 + gate * (1.0 - sigmoid_gate))).astype(
            jnp.bfloat16
        )
        d_up = (back * activated).astype(jnp.bfloat16)
        grads[0] += contract_first(key_norm, d_gate)
        grads[1] += contract_first(key_norm, d_up)
        grads[2] += contract_first(hidden, scaled)

    def both_ways(distance, action):
        @pl.when(z - distance >= 0)
        def _():
            action(z - distance)

        @pl.when(z + distance < depth)
        def _():
            action(z + distance)

    def pass_on(*pieces):
        def action(zp):
            for piece in pieces:
                arrive(zp * PAIR + x, piece)
                each_hop(zp, piece, start)

        return action

    def turned(zp):
        return ((zp == 0) & (z < depth - 1)) | ((zp == depth - 1) & (z > 0))

    def pass_detour(zp):
        @pl.when(turned(zp))
        def _():
            arrive(zp * PAIR + other, 1)

        each_detour(zp, start)

    def step(t, carry):
        code = at_place(mine, t)
        own_column = code % 2 == 1
        zp = code // 2
        slot = zp * PAIR + jnp.where(own_column, x, other)

        @pl.when(t == 1)
        def _():
            both_ways(1, pass_on(0))
            pass_detour(z)

        @pl.when((t % 2 == 1) & (t > 1))
        def _():
            both_ways((t - 1) // 2, pass_detour)

        @pl.when(t % 2 == 1)
        def _():
            both_ways((t + 1) // 2, pass_on(1))

        @pl.when((t % 2 == 0) & (t > 0))
        def _():
            both_ways(t // 2 + 1, pass_on(0))

        @pl.when(jnp.logical_not(own_column))
        def _():
            arrive(slot, 0)

            @pl.when(jnp.logical_not(turned(zp)))
            def _():
                arrive(slot, 1)

        @pl.when(slot <= me)
        def _():
            attend(slot)

        learn(slot)
        return carry

    lax.fori_loop(0, n_tok, step, 0)

    for m in range(3):
        summed = grads[m]
        norm = jnp.sqrt(jnp.sum(jnp.sum(summed * summed, axis=0, keepdims=True), axis=1, keepdims=True))
        ortho[m] = (summed / (norm + eps)).astype(jnp.bfloat16)

    def sweep(index, carry):
        for m in range(3):
            gram_ref[m] = contract_last(ortho[m], ortho[m]).astype(jnp.bfloat16)
        for m in range(3):
            cross_ref[m] = matmul(gram_ref[m], ortho[m]).astype(jnp.bfloat16)
        for m in range(3):
            square = matmul(gram_ref[m], cross_ref[m])
            ortho[m] = (
                ns_first * ortho[m].astype(jnp.float32)
                + ns_second * cross_ref[m].astype(jnp.float32)
                + ns_third * square
            ).astype(jnp.bfloat16)
        return carry

    lax.fori_loop(0, NS_STEPS, sweep, 0)

    def updated(m):
        return (
            w_ref[m].astype(jnp.float32) + update_rate * ortho[m].astype(jnp.float32)
        ).astype(jnp.bfloat16)

    query_norm = rms_norm(q_ref[...]).astype(jnp.bfloat16)
    gate = matmul(query_norm, updated(0))
    up_part = matmul(query_norm, updated(1))
    q_hidden = (jax.nn.silu(gate) * up_part).astype(jnp.bfloat16)
    applied = matmul(q_hidden, updated(2))
    attended = acc_ref[...] / total_ref[:, :1]
    heads_buf[head] = (attended + fw_scale * rms_norm(applied)).astype(jnp.bfloat16)

    def head_copy(block, sem, target):
        return pltpu.make_async_remote_copy(
            src_ref=heads_buf.at[block],
            dst_ref=heads_buf.at[block],
            send_sem=head_send.at[sem],
            recv_sem=head_recv.at[block],
            device_id={"head": target},
            device_id_type=MESH,
        )

    to_row = head_copy(head, 0, row_peer)
    to_core = head_copy(head, 1, core_peer)
    relay = head_copy(row_peer, 2, core_peer)
    corner = (core_peer + 2) % 4
    to_row.start()
    to_core.start()
    loads[2].wait()

    def project(block):
        first = pl.multiple_of(block * width, width)
        return matmul(heads_buf[block], ow_ref[pl.ds(first, width), :])

    projected = project(head)
    head_copy(core_peer, 1, core_peer).wait_recv()
    projected += project(core_peer)
    head_copy(row_peer, 0, row_peer).wait_recv()
    relay.start()
    projected += project(row_peer)
    head_copy(corner, 2, core_peer).wait_recv()
    projected += project(corner)
    result[...] = projected.astype(result.dtype)

    to_row.wait_send()
    to_core.wait_send()
    relay.wait_send()

    def finish(copy):
        copy.wait_send()

    def drain(zp, carry):
        for piece in (0, 1):
            each_hop(zp, piece, finish)
        each_detour(zp, finish)
        return carry

    lax.fori_loop(0, depth, drain, 0)


def fused_body(queries, key_rows, value_rows, learn_rates, fast_weights, out_weight):
    rows, width = queries.shape
    n_tok = lax.axis_size("tok")
    n_head = lax.axis_size("head")
    columns = out_weight.shape[1]
    dma = pltpu.SemaphoreType.DMA
    return pl.pallas_call(
        functools.partial(fused_kernel, n_tok),
        out_shape=jax.ShapeDtypeStruct((rows, columns), jnp.bfloat16),
        in_specs=[pl.BlockSpec(memory_space=pl.ANY)] * 6,
        out_specs=pl.BlockSpec(memory_space=pltpu.VMEM),
        scratch_shapes=[
            pltpu.VMEM((rows, width), jnp.bfloat16),
            pltpu.VMEM((n_tok, rows, width), jnp.bfloat16),
            pltpu.VMEM((n_tok, width + 16, rows), jnp.bfloat16),
            pltpu.VMEM((1, rows), jnp.float32),
            pltpu.VMEM(fast_weights.shape[1:], jnp.bfloat16),
            pltpu.VMEM(out_weight.shape, jnp.bfloat16),
            pltpu.VMEM(fast_weights.shape[1:], jnp.float32),
            pltpu.VMEM(fast_weights.shape[1:], jnp.bfloat16),
            pltpu.VMEM(fast_weights.shape[1:], jnp.bfloat16),
            pltpu.VMEM(fast_weights.shape[1:], jnp.bfloat16),
            pltpu.VMEM((rows, 128), jnp.float32),
            pltpu.VMEM((rows, 128), jnp.float32),
            pltpu.VMEM((rows, width), jnp.float32),
            pltpu.VMEM((n_head, rows, width), jnp.bfloat16),
            dma((5 + width // rows,)),
            dma((n_tok, 2)),
            dma((n_tok, 2)),
            dma((n_tok, 2)),
            dma((n_tok, 2)),
            dma((n_head,)),
            dma((3,)),
        ],
        compiler_params=pltpu.CompilerParams(
            collective_id=0, has_side_effects=True
        ),
    )(queries, key_rows, value_rows, learn_rates.reshape(1, rows), fast_weights, out_weight)


def block_attend(query_block, key_block, value_block, offset):
    scores = contract_last(query_block, key_block) * HD ** (-0.5)
    row_ids = lax.broadcasted_iota(jnp.int32, scores.shape, 0)
    col_ids = lax.broadcasted_iota(jnp.int32, scores.shape, 1)
    allowed = (col_ids > row_ids) & (col_ids <= row_ids + WIN) & (col_ids >= WIN - offset)
    scores = jnp.where(allowed, scores, -jnp.inf)
    top_score = jnp.max(scores, axis=1, keepdims=True)
    weights = jnp.exp(scores - top_score)
    totals = jnp.sum(weights, axis=1, keepdims=True)
    probs = (weights / totals).astype(jnp.bfloat16)
    return jnp.dot(probs, value_block, preferred_element_type=jnp.float32)


def fast_grads(key_part, value_part, rate_part, weights):
    key_norm = rms_norm(key_part).astype(jnp.bfloat16)
    gate = jnp.dot(key_norm, weights[0], preferred_element_type=jnp.float32)
    up_part = jnp.dot(key_norm, weights[1], preferred_element_type=jnp.float32)
    sigmoid_gate = jax.nn.sigmoid(gate)
    activated = gate * sigmoid_gate
    hidden = (activated * up_part).astype(jnp.bfloat16)
    scaled = (rate_part[:, None] * value_part.astype(jnp.float32)).astype(jnp.bfloat16)
    back = contract_last(scaled, weights[2])
    d_gate = (back * up_part * sigmoid_gate * (1.0 + gate * (1.0 - sigmoid_gate))).astype(
        jnp.bfloat16
    )
    d_up = (back * activated).astype(jnp.bfloat16)
    return jnp.stack(
        [
            contract_first(key_norm, d_gate),
            contract_first(key_norm, d_up),
            contract_first(hidden, scaled),
        ]
    )


def fast_apply(query_part, weights):
    query_norm = rms_norm(query_part).astype(jnp.bfloat16)
    gate = jnp.dot(query_norm, weights[0], preferred_element_type=jnp.float32)
    up_part = jnp.dot(query_norm, weights[1], preferred_element_type=jnp.float32)
    q_hidden = (jax.nn.silu(gate) * up_part).astype(jnp.bfloat16)
    return jnp.dot(q_hidden, weights[2], preferred_element_type=jnp.float32)


def body(queries, key_rows, value_rows, learn_rates, fast_weights, out_weight):
    tok_rows = queries.shape[0]
    reach_shards = WIN // tok_rows
    offset = lax.axis_index("tok") * tok_rows
    stacked = jnp.stack([key_rows, value_rows])
    earlier = []
    moving = stacked
    for distance in range(reach_shards):
        moving = passed_along(moving, "tok", 1)
        earlier.insert(0, moving)
    window_pairs = jnp.concatenate(earlier + [stacked], axis=1)
    weights = fast_weights[0]
    local_grads = fast_grads(key_rows, value_rows, learn_rates[:, 0], weights)
    attended = block_attend(queries, window_pairs[0], window_pairs[1], offset)
    summed = lax.psum(local_grads, "tok")
    norms = jnp.sqrt(jnp.sum(summed * summed, axis=(1, 2), keepdims=True))
    iterate = (summed / (norms + eps)).astype(jnp.bfloat16)
    for sweep in range(NS_STEPS):
        gram = jnp.einsum(
            "mij,mkj->mik", iterate, iterate, preferred_element_type=jnp.float32
        ).astype(jnp.bfloat16)
        cross = jnp.einsum(
            "mik,mkj->mij", gram, iterate, preferred_element_type=jnp.float32
        ).astype(jnp.bfloat16)
        square = jnp.einsum("mik,mkj->mij", gram, cross, preferred_element_type=jnp.float32)
        iterate = (
            ns_first * iterate.astype(jnp.float32)
            + ns_second * cross.astype(jnp.float32)
            + ns_third * square
        ).astype(jnp.bfloat16)
    updated = (weights.astype(jnp.float32) + update_rate * iterate.astype(jnp.float32)).astype(
        jnp.bfloat16
    )
    applied = fast_apply(queries, updated)
    mixed = (attended + fw_scale * rms_norm(applied)).astype(jnp.bfloat16)
    projected = jnp.dot(
        lax.all_gather(mixed, "head", axis=1, tiled=True),
        out_weight,
        preferred_element_type=jnp.float32,
    )
    return projected.astype(jnp.bfloat16)


def solution(mesh):
    placed = (
        P("tok", "head"),
        P("tok", "head"),
        P("tok", "head"),
        P("tok", "head"),
        P("head", None, None, None),
        P(None, "head"),
    )

    def chosen(queries, *others):
        whole_window = queries.shape[0] * mesh.shape["tok"] <= WIN
        square = mesh.shape["head"] == PAIR * PAIR and mesh.shape["tok"] % PAIR == 0
        return (fused_body if whole_window and square else body)(queries, *others)

    return jax.shard_map(
        chosen, mesh=mesh, in_specs=placed, out_specs=P("tok", "head"), check_vma=False
    )
```

profile of v0, /device:TPU:1, one launch (start us, length us, event | category | flops | bytes accessed | tf_op | source)
XLA Modules:
  0.0 43.0 jit_solution(15112919020189959622)
XLA Ops:
  0.0 41.4 %shard_map.64 = bf16[128,512]{1,0:T(8,128)(2,1)} custom-call(bf16[128,512]{1,0:T(8,128)(2,1)} %q_hbm.1, bf16[128,512]{1,0:T(8,128)(2,1)} %k_hbm.1, bf16[128,512]{1,0:T(8,128)(2,1)} %v_hbm.1, f32[1,128]{1,0:T(1,128)} %bitcast.1, bf16[1,3,512,512]{3,2,1,0:T(8,128)(2,1)} %weights_hbm.1, bf16[2048,512]{1,0:T(8,128)(2,1)} %out_hbm.1), custom_call_target="tpu_custom_call" | custom-call | tf_op jit(solution)/shard_map/pallas_call | solution.py:407
  41.4 1.6 %copy.8 = bf16[128,512]{1,0:T(8,128)(2,1)} copy(bf16[128,512]{1,0:T(8,128)(2,1)} %shard_map.64) | data formatting | bytes 262144
where the time goes:
time: 43.1 us; the launch traced here: 43 us
  Pallas kernels  41.4 us (96%)
  local copies, waits for them, and re-layouts  1.57 us (4%)
    pallas_call x1, Pallas kernels, fused_body(): pl.pallas_call(functools.partial(fused_kernel, n_tok), out_shape=jax.Shap...  41.4 us
    unnamed x1, local copies, waits for them, and re-layouts  1.57 us

commit v1 on v0

--- a/solution.py
+++ b/solution.py
@@ -433,9 +433,9 @@
             dma((3,)),
         ],
         compiler_params=pltpu.CompilerParams(
-            collective_id=0, has_side_effects=True
+            collective_id=0, has_side_effects=True, vmem_limit_bytes=48*1024*1024
         ),
-    )(queries, key_rows, value_rows, learn_rates.reshape(1, rows), fast_weights, out_weight)
+    )(*[pltpu.with_memory_space_constraint(a, pltpu.HBM) for a in (queries, key_rows, value_rows, learn_rates.reshape(1, rows), fast_weights, out_weight)])
 
 
 def block_attend(query_block, key_block, value_block, offset):

time: 43.1 us -> 41.6 us (0.965)
  local copies, waits for them, and re-layouts: 1.57 us -> 0.66 us
  Pallas kernels: 41.4 us -> 40.7 us
    unnamed x1, local copies, waits for them, and re-layouts: 1.57 us -> 0.66 us
    pallas_call x1, Pallas kernels: 41.4 us -> 40.7 us  [fused_body(): pl.pallas_call(functools.partial(fused_kernel, n_tok), out_shape=jax.Shap...]
where the time goes in v1:
time: 41.6 us; the launch traced here: 41.4 us
  Pallas kernels  40.7 us (98%)
  local copies, waits for them, and re-layouts  0.66 us (2%)
    pallas_call x1, Pallas kernels, fused_body(): pl.pallas_call(functools.partial(fused_kernel, n_tok), out_shape=jax.Shap...  40.7 us

profile of v1, /device:TPU:1, one launch (start us, length us, event | category | flops | bytes accessed | tf_op | source)
XLA Modules:
  0.0 41.4 jit_solution(9630478246950696692)
XLA Ops:
  0.0 40.7 %shard_map.64 = bf16[128,512]{1,0:T(8,128)(2,1)S(1)} custom-call(bf16[128,512]{1,0:T(8,128)(2,1)} %q_hbm.1, bf16[128,512]{1,0:T(8,128)(2,1)} %k_hbm.1, bf16[128,512]{1,0:T(8,128)(2,1)} %v_hbm.1, f32[1,128]{1,0:T(1,128)} %bitcast.1, bf16[1,3,512,512]{3,2,1,0:T(8,128)(2,1)} %weights_hbm.1, bf16[2048,512]{1,0:T(8,128)(2,1)} %out_hbm.1), custom_call_target="tpu_custom_call" | custom-call | tf_op jit(solution)/shard_map/pallas_call | solution.py:407
  40.8 0.7 %copy.8 = bf16[128,512]{1,0:T(8,128)(2,1)} copy(bf16[128,512]{1,0:T(8,128)(2,1)S(1)} %shard_map.64) | data formatting | bytes 262144
